TPU v7x, 256 devices: a whole 4x4x8 slice. The times are simulated.
256 devices in a mesh: dp: 32 (over z, y), block: 8 (over x, core).
Axes of the slice: x: 4, y: 4, z: 8, core: 2. Of those that a mesh axis runs over, the one named last changes fastest.
Arguments:
- x_act: bfloat16 [8, 16384, 4096], P('block', 'dp')
- g_out: bfloat16 [8, 16384, 4096], P('block', 'dp')
- proj_in: bfloat16 [8, 4096, 64], P('block'), may hold values from -0.09375 to 0.09375
- proj_out: bfloat16 [8, 4096, 64], P('block'), may hold values from -0.09375 to 0.09375
- queries: bfloat16 [8, 2048, 4096], P('block', 'dp'), may hold values from -6 to 6
- cand_ids: int32 [32, 32, 2], P('dp'), may hold values from 0 to 15, as said below
- cand_counts: int32 [32, 32], P('dp'), may hold values from 0 to 2, as said below
Outputs:
- scores: float32 [2048, 128], P(('dp', 'block'))
Inputs may be any that keep to these rules, and one draw needn't show every extreme that they name: `cand_ids`: each list of a training shard d for an owner p names 2 distinct query blocks of p; slots at or past cand_counts[d, p] are padding. Every training shard d has cand_counts[d, d] = 2.
All inputs are finite; a program needn't handle non-finite values.
Results may differ from a plain program's by a relative error of at most 0.0096.
Values may be sent and summed in bfloat16 or wider, within the bound.
No kernel may reach another device: no remote copies, remote signals or barrier semaphores. Data moves between devices by JAX's collectives and lax.ppermute only.
A program may use at most 64 MiB of HBM per device.

v0:
```python
import jax
import jax.numpy as jnp
from jax import lax
from jax.sharding import PartitionSpec as P

E_DEV = 4
SEQ = 128
QB = 4
CAP = 2
DAMP = 0.1


def kron_inverse(factor):
    width = factor.shape[0]
    identity = jnp.eye(width, dtype=jnp.float32)
    damping = DAMP * jnp.trace(factor) / width + 1e-06
    lower_factor = jnp.linalg.cholesky(factor + damping * identity)
    return jax.scipy.linalg.cho_solve((lower_factor, True), identity)


def body(x_act, g_out, proj_in, proj_out, queries, cand_ids, cand_counts):
    act_rows = x_act[0]
    grad_rows = g_out[0]
    row_count = act_rows.shape[0]
    width = proj_in.shape[2]
    n_owners = lax.axis_size("dp")
    n_layers = lax.axis_size("block")
    act_proj = jnp.dot(act_rows, proj_in[0], preferred_element_type=jnp.float32).astype(
        jnp.bfloat16
    )
    grad_proj = jnp.dot(grad_rows, proj_out[0], preferred_element_type=jnp.float32).astype(
        jnp.bfloat16
    )
    contract_rows = (((0,), (0,)), ((), ()))
    part_a = lax.dot_general(act_proj, act_proj, contract_rows, preferred_element_type=jnp.float32)
    part_g = lax.dot_general(
        grad_proj, grad_proj, contract_rows, preferred_element_type=jnp.float32
    )
    factor_a, factor_g = lax.psum((part_a, part_g), "dp")
    token_total = row_count * n_owners
    inverse_a = kron_inverse(factor_a / token_total)
    inverse_g = kron_inverse(factor_g / token_total)
    act_three = act_proj.reshape(E_DEV, SEQ, width)
    grad_three = grad_proj.reshape(E_DEV, SEQ, width)
    example_grad = (
        jnp.einsum("esi,esj->eij", grad_three, act_three, preferred_element_type=jnp.float32) / SEQ
    )
    left_side = jnp.einsum("ij,ejk->eik", inverse_g, example_grad, precision=lax.Precision.HIGHEST)
    precond = jnp.einsum("eik,kl->eil", left_side, inverse_a, precision=lax.Precision.HIGHEST)
    precond = precond.reshape(E_DEV, width * width).astype(jnp.bfloat16)
    req_ids, req_counts = (
        lax.all_to_all(cand_ids, "dp", split_axis=1, concat_axis=0, tiled=True),
        lax.all_to_all(cand_counts, "dp", split_axis=1, concat_axis=0, tiled=True),
    )
    req_ids = req_ids.reshape(n_owners, CAP)
    req_counts = req_counts.reshape(n_owners)
    query_rows = queries[0]
    owned = query_rows.shape[0]
    block_count = owned // QB
    slot_live = jnp.arange(CAP)[None, :] < req_counts[:, None]
    onehot = (
        (req_ids[:, :, None] == jnp.arange(block_count)[None, None, :]) & slot_live[:, :, None]
    ).astype(jnp.float32)
    dense_part = lax.dot_general(
        query_rows,
        lax.all_gather(precond, "dp", axis=0, tiled=True),
        (((1,), (1,)), ((), ())),
        preferred_element_type=jnp.float32,
    )
    live_blocks = jnp.sum(onehot, axis=1)
    mask_full = jnp.broadcast_to(
        jnp.transpose(live_blocks)[:, None, :, None], (block_count, QB, n_owners, E_DEV)
    ).reshape(owned, n_owners * E_DEV)
    layer_part = dense_part * mask_full
    scale = 1.0 / float(width * width * n_layers) ** 0.5
    return lax.psum_scatter(layer_part * scale, "block", scatter_dimension=0, tiled=True)


def solution(mesh):
    return jax.shard_map(
        body,
        mesh=mesh,
        in_specs=(
            P("block", "dp", None),
            P("block", "dp", None),
            P("block", None, None),
            P("block", None, None),
            P("block", "dp", None),
            P("dp", None, None),
            P("dp", None),
        ),
        out_specs=P(("dp", "block"), None),
        check_vma=False,
    )
```

profile of v0, /device:TPU:64, one launch (start us, length us, event | category | flops | bytes accessed | tf_op | source)
XLA Modules:
  0.0 291.4 jit_solution(2975817334751202043)
XLA Ops:
  6.5 0.0 copy-start
  6.5 1.0 copy-done
  7.6 3.7 %fusion.4 = bf16[512,64]{0,1:T(8,128)(2,1)S(1)} fusion(bf16[1,512,4096]{2,1,0:T(8,128)(2,1)} %param.11, bf16[1,4096,64]{1,2,0:T(8,128)(2,1)S(1)} %copy-done), kind=kOutput, calls=%fused_computation.6 | convolution fusion | flops 268468224 | bytes 4784128 | tf_op jit(solution)/shard_map/dot_general | solution.py:31
  11.3 0.0 copy-start.5
  11.3 0.0 copy-start.4
  11.3 0.0 copy-start.6
  11.3 0.1 fusion.32
  11.5 1.4 fusion.7
  12.9 0.0 copy-start.3
  12.9 0.1 fusion.33
  13.1 0.2 convolution_multiply_fusion
  13.2 133.0 %all-reduce.1 = (f32[64,64]{0,1:T(8,128)S(1)}, f32[64,64]{0,1:T(8,128)S(1)}) all-reduce(f32[64,64]{0,1:T(8,128)S(1)} %fusion.32, f32[64,64]{0,1:T(8,128)S(1)} %fusion.33), channel_id=1, replica_groups=mesh['dp'=32,'block'=8] {'dp'}, use_global_device_ids=true, to_apply=%region_0.0 | all-reduce | flops 8192 | bytes 65536 | tf_op jit(solution)/shard_map/psum | solution.py:39
  146.2 0.7 select_reduce_fusion.3
  146.9 0.6 select_reduce_fusion.2
  148.9 0.1 copy.48
  149.0 5.8 %cholesky.55 = f32[64,64]{1,0:T(8,128)S(1)} custom-call(f32[64,64]{1,0:T(8,128)S(1)} %fusion.27), custom_call_target="Cholesky" | custom-call | tf_op jit(solution)/shard_map/jit(cholesky)/cholesky | solution.py:17
  154.9 0.6 compare_reduce_fusion
  155.5 0.7 fusion.24
  156.2 4.9 %custom-call.9 = f32[1,64,64]{1,2,0:T(8,128)S(1)} custom-call(f32[1,64,64]{2,1,0:T(8,128)S(1)} %fusion.24), custom_call_target="InvertDiagBlocksLowerTriangular" | custom-call | tf_op jit(solution)/shard_map/jit(_cho_solve)/triangular_solve | solution.py:18
  161.1 0.3 fusion.19
  161.3 0.2 convolution_bitcast_fusion.2
  161.5 0.1 copy.45
  161.6 5.8 %cholesky.44 = f32[64,64]{1,0:T(8,128)S(1)} custom-call(f32[64,64]{1,0:T(8,128)S(1)} %fusion.30), custom_call_target="Cholesky" | custom-call | tf_op jit(solution)/shard_map/jit(cholesky)/cholesky | solution.py:17
  167.5 0.6 compare_reduce_fusion.1
  168.1 0.7 fusion.23
  168.8 4.9 %custom-call.8 = f32[1,64,64]{1,2,0:T(8,128)S(1)} custom-call(f32[1,64,64]{2,1,0:T(8,128)S(1)} %fusion.23), custom_call_target="InvertDiagBlocksLowerTriangular" | custom-call | tf_op jit(solution)/shard_map/jit(_cho_solve)/triangular_solve | solution.py:18
  173.7 0.3 fusion.21
  173.9 0.2 convolution_bitcast_fusion.3
  174.1 0.4 convolution_bitcast_fusion
  174.5 0.4 convolution_convert_fusion
  174.9 0.7 reshape.60
  175.6 0.0 all-gather.3.cloned.1.call-update
  175.6 0.7 copy.52
  176.3 16.2 %all-to-all-start.1 = ((s32[1,32,1]{2,0,1:T(1,128)}), s32[1,32,1]{2,0,1:T(1,128)S(1)}, u32[]{:S(2)}, u32[]{:S(2)}) async-start(s32[1,32,1]{2,0,1:T(1,128)} %copy.52), calls=%async_computation.1 | async-start | bytes 32768 | tf_op jit(solution)/shard_map/all_to_all | solution.py:53
  192.5 0.7 copy.50
  193.2 0.6 dynamic-slice
  194.4 5.8 %all-to-all-done.1 = s32[1,32,1]{2,0,1:T(1,128)S(1)} async-done(((s32[1,32,1]{2,0,1:T(1,128)}), s32[1,32,1]{2,0,1:T(1,128)S(1)}, u32[]{:S(2)}, u32[]{:S(2)}) %all-to-all-start.1) | async-done | bytes 160 | tf_op jit(solution)/shard_map/all_to_all | solution.py:53
  200.3 5.6 %all-to-all-start = ((s32[1,32,2]{2,0,1:T(1,128)}), s32[1,32,2]{2,0,1:T(1,128)S(1)}, u32[]{:S(2)}, u32[]{:S(2)}) async-start(s32[1,32,2]{2,0,1:T(1,128)} %copy.50), calls=%async_computation | async-start | bytes 32768 | tf_op jit(solution)/shard_map/all_to_all | solution.py:52
  205.9 0.7 reduce.4
  206.5 7.1 %all-to-all-done = s32[1,32,2]{2,0,1:T(1,128)S(1)} async-done(((s32[1,32,2]{2,0,1:T(1,128)}), s32[1,32,2]{2,0,1:T(1,128)S(1)}, u32[]{:S(2)}, u32[]{:S(2)}) %all-to-all-start) | async-done | bytes 288 | tf_op jit(solution)/shard_map/all_to_all | solution.py:52
  213.6 0.1 copy.51
  213.7 0.2 broadcast_in_dim.9
  213.9 0.6 reshape.59
  214.6 43.9 %all-gather.3.cloned.1.call-done = bf16[32,4,4096]{2,1,0:T(4,128)(2,1)} async-done(((bf16[1,4,4096]{2,1,0:T(4,128)(2,1)}), bf16[32,4,4096]{2,1,0:T(4,128)(2,1)}) %all-gather.3.cloned.1.call-update) | async-done | bytes 1048592 | tf_op jit(solution)/shard_map/all_gather | solution.py:66
  258.5 1.3 reshape.61
  259.9 0.5 fusion.11
  260.4 23.6 %all-reduce = f32[64,128]{1,0:T(8,128)S(1)} all-reduce(f32[64,128]{1,0:T(8,128)S(1)} %fusion.11), channel_id=2, replica_groups=mesh['dp'=32,'block'=8] {'block'}, use_global_device_ids=true, to_apply=%region_7.10.clone | all-reduce | flops 8192 | bytes 65536
  284.0 0.6 constant_dynamic-slice_fusion
  (16 shorter events, 0.1 us)
Async XLA Ops:
  6.5 1.0 copy-start
  6.5 5.0 %copy-start.2 = (bf16[1,4096,64]{1,2,0:T(8,128)(2,1)S(1)}, bf16[1,4096,64]{1,2,0:T(8,128)(2,1)}, u32[]{:S(2)}) copy-start(bf16[1,4096,64]{1,2,0:T(8,128)(2,1)} %param.12) | copy-start | bytes 1572868
  6.5 252.0 %all-gather.3.cloned.1.call-start = ((), (), s32[]{:S(2)}) async-start(), calls=%async_computation.2 | async-start | bytes 1081344 | tf_op jit(solution)/shard_map/all_gather | solution.py:66
  7.6 3.9 %copy-start.1 = (bf16[1,512,4096]{2,1,0:T(8,128)(2,1)S(1)}, bf16[1,512,4096]{2,1,0:T(8,128)(2,1)}, u32[]{:S(2)}) copy-start(bf16[1,512,4096]{2,1,0:T(8,128)(2,1)} %param.10) | copy-start | bytes 12582916
  11.3 164.3 %copy-start.5 = (s32[1,32]{1,0:T(1,128)S(1)}, s32[1,32]{1,0:T(1,128)}, u32[]{:S(2)}) copy-start(s32[1,32]{1,0:T(1,128)} %param.16) | copy-start | bytes 388
  11.3 181.2 %copy-start.4 = (s32[1,32,2]{1,2,0:T(2,128)S(1)}, s32[1,32,2]{1,2,0:T(2,128)}, u32[]{:S(2)}) copy-start(s32[1,32,2]{1,2,0:T(2,128)} %param.15) | copy-start | bytes 772
  11.3 181.9 %copy-start.6 = (u32[256]{0:T(256)S(1)}, u32[256]{0:T(256)}, u32[]{:S(2)}) copy-start(u32[256]{0:T(256)} %constant.72) | copy-start | bytes 3076
  12.9 247.0 %copy-start.3 = (bf16[1,64,4096]{2,1,0:T(8,128)(2,1)S(1)}, bf16[1,64,4096]{2,1,0:T(8,128)(2,1)}, u32[]{:S(2)}) copy-start(bf16[1,64,4096]{2,1,0:T(8,128)(2,1)} %param.14) | copy-start | bytes 1572868
  176.3 24.0 %all-to-all-start.1 = ((s32[1,32,1]{2,0,1:T(1,128)}), s32[1,32,1]{2,0,1:T(1,128)S(1)}, u32[]{:S(2)}, u32[]{:S(2)}) async-start(s32[1,32,1]{2,0,1:T(1,128)} %copy.52), calls=%async_computation.1 | async-start | bytes 32768 | tf_op jit(solution)/shard_map/all_to_all | solution.py:53
  200.3 13.4 %all-to-all-start = ((s32[1,32,2]{2,0,1:T(1,128)}), s32[1,32,2]{2,0,1:T(1,128)S(1)}, u32[]{:S(2)}, u32[]{:S(2)}) async-start(s32[1,32,2]{2,0,1:T(1,128)} %copy.50), calls=%async_computation | async-start | bytes 32768 | tf_op jit(solution)/shard_map/all_to_all | solution.py:52
Sparse Core Ops, SparseCore 0:
  175.7 82.7 all-gather.2
where the time goes:
time: 292 us; the launch traced here: 291 us
  blocking collectives  157 us (54%)
  waiting for transfers between devices  56.9 us (19%)
  other arithmetic  26.1 us (9%)
  starting transfers between devices  21.8 us (7%)
  between operations  15.6 us (5%)
  matrix products  7.64 us (3%)
  local copies, waits for them, and re-layouts  6.72 us (2%)
    psum x1, blocking collectives, body(): factor_a, factor_g = lax.psum((part_a, part_g), 'dp')  133 us
    all_gather x1, waiting for transfers between devices, body(): lax.all_gather(precond, 'dp', axis=0, tiled=True)  43.9 us
    unnamed x1, blocking collectives  23.6 us
    all_to_all x1, starting transfers between devices, body(): lax.all_to_all(cand_counts, 'dp', split_axis=1, concat_axis=0, tiled=True)  16.2 us
    another operation x6, other arithmetic, kron_inverse(): lower_factor = jnp.linalg.cholesky(factor + damping * identity)  13 us
    another operation x4, other arithmetic, kron_inverse(): return jax.scipy.linalg.cho_solve((lower_factor, True), identity)  11.1 us
    all_to_all x1, waiting for transfers between devices, body(): lax.all_to_all(cand_ids, 'dp', split_axis=1, concat_axis=0, tiled=True)  7.09 us
  transfers between devices with their start and end apart: 3, of which 3 were waited for; matrix products, arithmetic and copies ran while one was open for 1% of the time, Pallas kernels for 0%

commit v1 on v0

--- a/solution.py
+++ b/solution.py
@@ -63,7 +63,9 @@
     ).astype(jnp.float32)
     dense_part = lax.dot_general(
         query_rows,
-        lax.all_gather(precond, "dp", axis=0, tiled=True),
+        jnp.concatenate(
+            lax.all_to_all(jnp.stack([precond] * lax.axis_size("dp")), "dp", 0, 0), axis=0
+        ),
         (((1,), (1,)), ((), ())),
         preferred_element_type=jnp.float32,
     )

time: 292 us -> 254 us (0.87)
  waiting for transfers between devices: 56.9 us -> 22.7 us
  between operations: 15.6 us -> 2.13 us
  starting transfers between devices: 21.8 us -> 34.1 us
  blocking collectives: 157 us -> 154 us
    all_gather x1 -> x0, waiting for transfers between devices: 43.9 us -> none  [body(): lax.all_gather(precond, 'dp', axis=0, tiled=True)]
    all_to_all x0 -> x1, waiting for transfers between devices: none -> 15.5 us  [body(): lax.all_to_all(jnp.stack([precond] * lax.axis_size('dp')), 'dp', 0, 0)]
    all_to_all x1, starting transfers between devices: 5.59 us -> 17.3 us  [body(): lax.all_to_all(cand_ids, 'dp', split_axis=1, concat_axis=0, tiled=True)]
    all_to_all x0 -> x1, starting transfers between devices: none -> 5.91 us  [body(): lax.all_to_all(jnp.stack([precond] * lax.axis_size('dp')), 'dp', 0, 0)]
    all_to_all x1, waiting for transfers between devices: 5.84 us -> 0.01 us  [body(): lax.all_to_all(cand_counts, 'dp', split_axis=1, concat_axis=0, tiled=True)]
    all_to_all x1, starting transfers between devices: 16.2 us -> 10.9 us  [body(): lax.all_to_all(cand_counts, 'dp', split_axis=1, concat_axis=0, tiled=True)]
    unnamed x19 -> x15, local copies, waits for them, and re-layouts: 4.98 us -> 1.9 us
  transfers between devices with their start and end apart: 3 -> 3, of which waited for: 3 -> 2; matrix products, arithmetic and copies ran while one was open for 1% -> 14% of each run, Pallas kernels for 0% -> 0%
where the time goes in v1:
time: 254 us; the launch traced here: 253 us
  blocking collectives  154 us (61%)
  starting transfers between devices  34.1 us (13%)
  other arithmetic  26.1 us (10%)
  waiting for transfers between devices  22.7 us (9%)
  matrix products  7.65 us (3%)
  local copies, waits for them, and re-layouts  6.21 us (2%)
    psum x1, blocking collectives, body(): factor_a, factor_g = lax.psum((part_a, part_g), 'dp')  130 us
    unnamed x1, blocking collectives  23.6 us
    all_to_all x1, starting transfers between devices, body(): lax.all_to_all(cand_ids, 'dp', split_axis=1, concat_axis=0, tiled=True)  17.3 us
    all_to_all x1, waiting for transfers between devices, body(): lax.all_to_all(jnp.stack([precond] * lax.axis_size('dp')), 'dp', 0, 0)  15.5 us
    another operation x6, other arithmetic, kron_inverse(): lower_factor = jnp.linalg.cholesky(factor + damping * identity)  13 us
    another operation x4, other arithmetic, kron_inverse(): return jax.scipy.linalg.cho_solve((lower_factor, True), identity)  11.1 us
    all_to_all x1, starting transfers between devices, body(): lax.all_to_all(cand_counts, 'dp', split_axis=1, concat_axis=0, tiled=True)  10.9 us
    all_to_all x1, waiting for transfers between devices, body(): lax.all_to_all(cand_ids, 'dp', split_axis=1, concat_axis=0, tiled=True)  7.19 us
  transfers between devices with their start and end apart: 3, of which 2 were waited for; matrix products, arithmetic and copies ran while one was open for 14% of the time, Pallas kernels for 0%

profile of v1, /device:TPU:64, one launch (start us, length us, event | category | flops | bytes accessed | tf_op | source)
XLA Modules:
  0.0 253.0 jit_solution(6339354013856781801)
XLA Ops:
  0.0 1.4 copy.52
  1.4 10.9 %all-to-all-start.2 = ((s32[1,32,1]{2,0,1:T(1,128)}), s32[1,32,1]{2,0,1:T(1,128)S(1)}, u32[]{:S(2)}, u32[]{:S(2)}) async-start(s32[1,32,1]{2,0,1:T(1,128)} %copy.52), calls=%async_computation.2 | async-start | bytes 32768 | tf_op jit(solution)/shard_map/all_to_all | solution.py:53
  12.3 0.0 copy-start.1
  12.4 3.7 %fusion.4 = bf16[512,64]{0,1:T(8,128)(2,1)S(1)} fusion(bf16[1,512,4096]{2,1,0:T(8,128)(2,1)} %param.11, bf16[1,4096,64]{1,2,0:T(8,128)(2,1)S(1)} %copy-done), kind=kOutput, calls=%fused_computation.6 | convolution fusion | flops 268468224 | bytes 4784128 | tf_op jit(solution)/shard_map/dot_general | solution.py:31
  16.1 0.0 copy-start.4
  16.1 0.1 fusion.32
  16.3 0.0 copy-start.5
  16.3 1.4 fusion.7
  17.7 0.2 fusion.33
  17.8 0.2 convolution_multiply_fusion
  18.0 130.5 %all-reduce.1 = (f32[64,64]{0,1:T(8,128)S(1)}, f32[64,64]{0,1:T(8,128)S(1)}) all-reduce(f32[64,64]{0,1:T(8,128)S(1)} %fusion.32, f32[64,64]{0,1:T(8,128)S(1)} %fusion.33), channel_id=1, replica_groups=mesh['dp'=32,'block'=8] {'dp'}, use_global_device_ids=true, to_apply=%region_0.0 | all-reduce | flops 8192 | bytes 65536 | tf_op jit(solution)/shard_map/psum | solution.py:39
  148.5 0.6 select_reduce_fusion.3
  149.1 0.6 select_reduce_fusion.2
  150.9 0.1 copy.48
  151.0 5.8 %cholesky.55 = f32[64,64]{1,0:T(8,128)S(1)} custom-call(f32[64,64]{1,0:T(8,128)S(1)} %fusion.27), custom_call_target="Cholesky" | custom-call | tf_op jit(solution)/shard_map/jit(cholesky)/cholesky | solution.py:17
  156.9 0.6 compare_reduce_fusion
  157.5 0.7 fusion.24
  158.2 4.9 %custom-call.9 = f32[1,64,64]{1,2,0:T(8,128)S(1)} custom-call(f32[1,64,64]{2,1,0:T(8,128)S(1)} %fusion.24), custom_call_target="InvertDiagBlocksLowerTriangular" | custom-call | tf_op jit(solution)/shard_map/jit(_cho_solve)/triangular_solve | solution.py:18
  163.1 0.3 fusion.19
  163.4 0.1 copy.45
  163.4 5.8 %cholesky.44 = f32[64,64]{1,0:T(8,128)S(1)} custom-call(f32[64,64]{1,0:T(8,128)S(1)} %fusion.30), custom_call_target="Cholesky" | custom-call | tf_op jit(solution)/shard_map/jit(cholesky)/cholesky | solution.py:17
  169.3 0.6 compare_reduce_fusion.1
  170.0 0.7 fusion.23
  170.6 4.9 %custom-call.8 = f32[1,64,64]{1,2,0:T(8,128)S(1)} custom-call(f32[1,64,64]{2,1,0:T(8,128)S(1)} %fusion.23), custom_call_target="InvertDiagBlocksLowerTriangular" | custom-call | tf_op jit(solution)/shard_map/jit(_cho_solve)/triangular_solve | solution.py:18
  175.5 0.3 fusion.21
  175.8 0.0 copy-start.3
  175.8 0.2 convolution_bitcast_fusion.3
  176.0 0.4 convolution_bitcast_fusion
  176.4 0.2 convolution_bitcast_fusion.2
  176.5 0.7 copy.50
  177.2 0.0 all-to-all-done.2
  177.2 17.3 %all-to-all-start.1 = ((s32[1,32,2]{2,0,1:T(1,128)}), s32[1,32,2]{2,0,1:T(1,128)S(1)}, u32[]{:S(2)}, u32[]{:S(2)}) async-start(s32[1,32,2]{2,0,1:T(1,128)} %copy.50), calls=%async_computation.1 | async-start | bytes 32768 | tf_op jit(solution)/shard_map/all_to_all | solution.py:52
  194.5 0.4 convolution_convert_fusion
  194.9 0.1 convert_element_type.27
  195.0 7.2 %all-to-all-done.1 = s32[1,32,2]{2,0,1:T(1,128)S(1)} async-done(((s32[1,32,2]{2,0,1:T(1,128)}), s32[1,32,2]{2,0,1:T(1,128)S(1)}, u32[]{:S(2)}, u32[]{:S(2)}) %all-to-all-start.1) | async-done | bytes 288 | tf_op jit(solution)/shard_map/all_to_all | solution.py:52
  202.2 1.5 stack.2
  203.7 5.9 %all-to-all-start = ((bf16[32,4,4096]{2,1,0:T(4,128)(2,1)}), bf16[32,4,4096]{2,1,0:T(4,128)(2,1)S(1)}, u32[]{:S(2)}, u32[]{:S(2)}) async-start(bf16[32,4,4096]{2,1,0:T(4,128)(2,1)} %stack.2), calls=%async_computation | async-start | bytes 2097152 | tf_op jit(solution)/shard_map/all_to_all | solution.py:67
  209.6 0.0 copy-done.5
  209.6 0.6 dynamic-slice
  210.9 0.7 reduce.4
  211.5 0.1 copy.51
  211.6 0.2 broadcast_in_dim.9
  211.8 0.6 reshape.66
  212.5 15.5 %all-to-all-done = bf16[32,4,4096]{2,1,0:T(4,128)(2,1)S(1)} async-done(((bf16[32,4,4096]{2,1,0:T(4,128)(2,1)}), bf16[32,4,4096]{2,1,0:T(4,128)(2,1)S(1)}, u32[]{:S(2)}, u32[]{:S(2)}) %all-to-all-start) | async-done | bytes 1048608 | tf_op jit(solution)/shard_map/all_to_all | solution.py:67
  228.0 0.3 reshape.65
  228.3 0.5 fusion.11
  228.8 23.6 %all-reduce = f32[64,128]{1,0:T(8,128)S(1)} all-reduce(f32[64,128]{1,0:T(8,128)S(1)} %fusion.11), channel_id=2, replica_groups=mesh['dp'=32,'block'=8] {'block'}, use_global_device_ids=true, to_apply=%region_7.10.clone | all-reduce | flops 8192 | bytes 65536
  252.4 0.6 constant_dynamic-slice_fusion
  (14 shorter events, 0.1 us)
Async XLA Ops:
  0.0 12.3 %copy-start = (bf16[1,4096,64]{1,2,0:T(8,128)(2,1)S(1)}, bf16[1,4096,64]{1,2,0:T(8,128)(2,1)}, u32[]{:S(2)}) copy-start(bf16[1,4096,64]{1,2,0:T(8,128)(2,1)} %param.13) | copy-start | bytes 1572868
  0.0 16.3 %copy-start.2 = (bf16[1,4096,64]{1,2,0:T(8,128)(2,1)S(1)}, bf16[1,4096,64]{1,2,0:T(8,128)(2,1)}, u32[]{:S(2)}) copy-start(bf16[1,4096,64]{1,2,0:T(8,128)(2,1)} %param.12) | copy-start | bytes 1572868
  1.4 175.8 %all-to-all-start.2 = ((s32[1,32,1]{2,0,1:T(1,128)}), s32[1,32,1]{2,0,1:T(1,128)S(1)}, u32[]{:S(2)}, u32[]{:S(2)}) async-start(s32[1,32,1]{2,0,1:T(1,128)} %copy.52), calls=%async_computation.2 | async-start | bytes 32768 | tf_op jit(solution)/shard_map/all_to_all | solution.py:53
  12.3 3.9 %copy-start.1 = (bf16[1,512,4096]{2,1,0:T(8,128)(2,1)S(1)}, bf16[1,512,4096]{2,1,0:T(8,128)(2,1)}, u32[]{:S(2)}) copy-start(bf16[1,512,4096]{2,1,0:T(8,128)(2,1)} %param.10) | copy-start | bytes 12582916
  16.1 160.4 %copy-start.4 = (s32[1,32,2]{1,2,0:T(2,128)S(1)}, s32[1,32,2]{1,2,0:T(2,128)}, u32[]{:S(2)}) copy-start(s32[1,32,2]{1,2,0:T(2,128)} %param.15) | copy-start | bytes 772
  16.3 193.3 %copy-start.5 = (u32[256]{0:T(256)S(1)}, u32[256]{0:T(256)}, u32[]{:S(2)}) copy-start(u32[256]{0:T(256)} %constant.72) | copy-start | bytes 3076
  175.8 52.5 %copy-start.3 = (bf16[1,64,4096]{2,1,0:T(8,128)(2,1)S(1)}, bf16[1,64,4096]{2,1,0:T(8,128)(2,1)}, u32[]{:S(2)}) copy-start(bf16[1,64,4096]{2,1,0:T(8,128)(2,1)} %param.14) | copy-start | bytes 1572868
  177.2 25.0 %all-to-all-start.1 = ((s32[1,32,2]{2,0,1:T(1,128)}), s32[1,32,2]{2,0,1:T(1,128)S(1)}, u32[]{:S(2)}, u32[]{:S(2)}) async-start(s32[1,32,2]{2,0,1:T(1,128)} %copy.50), calls=%async_computation.1 | async-start | bytes 32768 | tf_op jit(solution)/shard_map/all_to_all | solution.py:52
  203.7 24.3 %all-to-all-start = ((bf16[32,4,4096]{2,1,0:T(4,128)(2,1)}), bf16[32,4,4096]{2,1,0:T(4,128)(2,1)S(1)}, u32[]{:S(2)}, u32[]{:S(2)}) async-start(bf16[32,4,4096]{2,1,0:T(4,128)(2,1)} %stack.2), calls=%async_computation | async-start | bytes 2097152 | tf_op jit(solution)/shard_map/all_to_all | solution.py:67
